TPU v7x, 32 devices: a whole 2x2x4 slice. The times are simulated.
32 devices in a mesh: ka: 4 (over y, x), rp: 8 (over z, core).
Axes of the slice: x: 2, y: 2, z: 4, core: 2. Of those that a mesh axis runs over, the one named last changes fastest.
Arguments:
- coupling_table: bfloat16 [512, 256, 1024], P('ka', 'rp'), may hold values from -0.016479492 to 0.016479492
- k_points: int32 [3, 2048], P(None, 'ka'), may hold values from 0 to 15
- re_vectors: int32 [3, 512], replicated, may hold values from -6 to 6
- rp_vectors: int32 [3, 256], P(None, 'rp'), may hold values from -6 to 6
- q_points: int32 [3, 2], replicated, may hold values from 0 to 15
Outputs:
- bloch_coupling: float32 [2048, 2048], P(('ka', 'rp'))
All inputs are finite; a program needn't handle non-finite values.
Results may differ from a plain program's by a relative error of at most 0.0022.
Values may be sent and summed in bfloat16 or wider, within the bound.
A program may use at most 64 MiB of HBM per device.

v0:
```python
import math
import jax
import jax.numpy as jnp
from jax import lax
from jax.sharding import PartitionSpec as P

NKG = 16


def phases(left, right):
    nested = (
        left[0][:, None] * right[0][None, :]
        + left[1][:, None] * right[1][None, :]
        + left[2][:, None] * right[2][None, :]
    )
    wrapped = jnp.mod(nested, NKG)
    angles = wrapped.astype(jnp.float32) * (2.0 * math.pi / NKG)
    return (jnp.cos(angles), jnp.sin(angles))


def per_device(coupling_table, k_points, re_vectors, rp_vectors, q_points):
    high = lax.Precision.HIGHEST
    local_rp = coupling_table.shape[1]
    entries = coupling_table.shape[2] // 2
    waves = q_points.shape[1]
    q_cos, q_sin = phases(q_points, rp_vectors)
    k_cos, k_sin = phases(k_points, re_vectors)
    k_cos = k_cos.astype(jnp.bfloat16)
    k_sin = k_sin.astype(jnp.bfloat16)
    local_re = coupling_table.shape[0]
    values = coupling_table.astype(jnp.float32).reshape(local_re, local_rp, 2, entries)
    real_in = values[:, :, 0, :]
    imag_in = values[:, :, 1, :]
    real_mid = jnp.einsum("qr,erm->eqm", q_cos, real_in, precision=high) - jnp.einsum(
        "qr,erm->eqm", q_sin, imag_in, precision=high
    )
    imag_mid = jnp.einsum("qr,erm->eqm", q_sin, real_in, precision=high) + jnp.einsum(
        "qr,erm->eqm", q_cos, imag_in, precision=high
    )
    stacked = jnp.stack(
        [real_mid.reshape(local_re, waves * entries), imag_mid.reshape(local_re, waves * entries)],
        axis=0,
    )
    reduced = lax.psum_scatter(stacked, "rp", scatter_dimension=2, tiled=True)
    fragment = lax.all_gather(reduced, "ka", axis=1, tiled=True)
    cos_part = k_cos.astype(jnp.float32)
    sin_part = k_sin.astype(jnp.float32)
    real_add = jnp.dot(
        cos_part, fragment[0], precision=high, preferred_element_type=jnp.float32
    ) - jnp.dot(sin_part, fragment[1], precision=high, preferred_element_type=jnp.float32)
    imag_add = jnp.dot(
        sin_part, fragment[0], precision=high, preferred_element_type=jnp.float32
    ) + jnp.dot(cos_part, fragment[1], precision=high, preferred_element_type=jnp.float32)
    combined = jnp.stack([real_add, imag_add], axis=1)
    moved = lax.all_to_all(combined, "rp", split_axis=0, concat_axis=2, tiled=True)
    return moved.reshape(moved.shape[0], 2 * waves * entries)


def solution(mesh):
    placed = (P("ka", "rp", None), P(None, "ka"), P(), P(None, "rp"), P())
    return jax.shard_map(
        per_device, mesh=mesh, in_specs=placed, out_specs=P(("ka", "rp"), None), check_vma=False
    )
```

profile of v0, /device:TPU:0, one launch (start us, length us, event | category | flops | bytes accessed | tf_op | source)
XLA Modules:
  0.0 146.7 jit_solution(4808768817966968522)
XLA Ops:
  6.5 0.8 slice_bitcast_fusion.8
  7.3 1.0 slice_reduce_fusion.2
  8.3 12.1 %copy.11 = bf16[128,32,1024]{0,2,1:T(8,128)(2,1)} copy(bf16[128,32,1024]{2,1,0:T(8,128)(2,1)} %param.5) | data formatting | bytes 16777216 | tf_op args[0]
  20.4 5.9 %fusion.52 = (bf16[128,32,1,512]{0,3,2,1:T(8,128)(2,1)}, bf16[128,32,1,512]{0,3,2,1:T(8,128)(2,1)}) fusion(bf16[128,32,2,512]{0,3,2,1:T(8,128)(2,1)} %bitcast.65), kind=kLoop, calls=%fused_computation.64 | loop fusion | bytes 16777216 | tf_op jit(solution)/shard_map/slice | solution.py:32
  26.3 8.0 %copy.17 = bf16[128,32,1,512]{3,1,0,2:T(8,128)(2,1)} copy(bf16[128,32,1,512]{0,3,2,1:T(8,128)(2,1)} %get-tuple-element.11) | data formatting | bytes 8388608
  34.3 0.1 fusion.50
  34.4 8.0 %copy.16 = bf16[128,32,1,512]{3,1,0,2:T(8,128)(2,1)} copy(bf16[128,32,1,512]{0,3,2,1:T(8,128)(2,1)} %get-tuple-element.10) | data formatting | bytes 8388608
  42.4 4.1 %fusion.2 = f32[2,128,512]{2,0,1:T(2,128)S(1)} fusion(bf16[128,32,1,512]{3,1,0,2:T(8,128)(2,1)} %copy.17, f32[2,32]{1,0:T(2,128)S(1)} %get-tuple-element.8), kind=kOutput, calls=%fused_computation.2 | convolution fusion | flops 50331648 | bytes 4718848 | tf_op jit(solution)/shard_map/qr,erm->eqm/dot_general | solution.py:34
  46.5 1.8 %fusion = f32[2,128,512]{2,0,1:T(2,128)S(1)} fusion(bf16[128,32,1,512]{3,1,0,2:T(8,128)(2,1)S(1)} %copy-done, f32[2,32]{1,0:T(2,128)S(1)} %cos.7), kind=kOutput, calls=%fused_computation | convolution fusion | flops 50331648 | bytes 4718848 | tf_op jit(solution)/shard_map/qr,erm->eqm/dot_general | solution.py:37
  48.3 1.8 %fusion.11 = f32[128,2,512]{2,1,0:T(2,128)S(1)} fusion(f32[2,128,512]{2,0,1:T(2,128)S(1)} %fusion.2, bf16[128,32,1,512]{3,1,0,2:T(8,128)(2,1)S(1)} %copy-done.1, f32[2,32]{1,0:T(2,128)S(1)} %cos.7), kind=kOutput, calls=%fused_computation.12 | convolution fusion | flops 50462720 | bytes 5243136 | tf_op jit(solution)/shard_map/qr,erm->eqm/dot_general | solution.py:34
  50.1 0.5 stack_reshape.6
  50.6 3.9 %fusion.17 = f32[128,2,512]{2,1,0:T(2,128)S(1)} fusion(f32[2,128,512]{2,0,1:T(2,128)S(1)} %fusion, bf16[128,32,1,512]{3,1,0,2:T(8,128)(2,1)} %copy.16, f32[2,32]{1,0:T(2,128)S(1)} %get-tuple-element.8), kind=kOutput, calls=%fused_computation.14 | convolution fusion | flops 50462720 | bytes 5243136 | tf_op jit(solution)/shard_map/qr,erm->eqm/dot_general | solution.py:37
  54.5 0.5 stack_reshape.7
  55.0 1.0 pad_maximum_fusion
  56.1 35.4 %reduce-scatter.2.cloned.1.call-done = f32[2,128,128]{2,1,0:T(8,128)} async-done(((f32[2,128,1024]{2,1,0:T(8,128)}), f32[2,128,128]{2,1,0:T(8,128)}) %reduce-scatter.2.cloned.1.call-update) | async-done | bytes 131088 | tf_op jit(solution)/shard_map/reduce_scatter | solution.py:44
  91.5 10.5 %all_gather.3 = f32[2,512,128]{2,1,0:T(8,128)S(1)} all-gather(f32[2,128,128]{2,1,0:T(8,128)} %reduce-scatter.2.cloned.1.call-done), channel_id=1, replica_groups=mesh['ka'=4,'rp'=8] {'ka'}, dimensions={1}, use_global_device_ids=true | all-gather | bytes 655360 | tf_op jit(solution)/shard_map/all_gather | solution.py:45
  102.0 4.5 %fusion.25 = f32[512,128]{1,0:T(8,128)S(1)} fusion(s32[512]{0:T(512)S(1)} %bitcast.84, s32[512]{0:T(512)S(1)} %bitcast.72, s32[512]{0:T(512)S(1)} %bitcast.88, s32[512]{0:T(512)S(1)} %bitcast.76, s32[512]{0:T(512)S(1)} %bitcast.80, s32[512]{0:T(512)S(1)} %bitcast.68, f32[2,512,128]{2,1,0:T(8,128)S(1)} %all_gather.3), kind=kOutput, calls=%fused_computation.27 | convolution fusion | flops 407633920 | bytes 536576 | tf_op jit(solution)/shard_map/dot_general | solution.py:48
  106.5 4.6 %fusion.26 = f32[512,128]{1,0:T(8,128)S(1)} fusion(s32[512]{0:T(512)S(1)} %bitcast.85, s32[512]{0:T(512)S(1)} %bitcast.73, s32[512]{0:T(512)S(1)} %bitcast.89, s32[512]{0:T(512)S(1)} %bitcast.77, s32[512]{0:T(512)S(1)} %bitcast.81, s32[512]{0:T(512)S(1)} %bitcast.69, f32[2,512,128]{2,1,0:T(8,128)S(1)} %all_gather.3), kind=kOutput, calls=%fused_computation.28 | convolution fusion | flops 407633920 | bytes 536576 | tf_op jit(solution)/shard_map/dot_general | solution.py:51
  111.1 4.8 %fusion.21 = f32[512,1,128]{2,0,1:T(8,128)S(1)} fusion(f32[512,128]{1,0:T(8,128)S(1)} %fusion.25, s32[512]{0:T(512)S(1)} %bitcast.86, s32[512]{0:T(512)S(1)} %bitcast.74, s32[512]{0:T(512)S(1)} %bitcast.90, s32[512]{0:T(512)S(1)} %bitcast.78, s32[512]{0:T(512)S(1)} %bitcast.82, s32[512]{0:T(512)S(1)} %bitcast.70, f32[2,512,128]{2,1,0:T(8,128)S(1)} %all_gather.3), kind=kOutput, calls=%fused_computation.18 | convolution fusion | flops 407699456 | bytes 798720 | tf_op jit(solution)/shard_map/dot_general | solution.py:50
  115.9 4.5 %fusion.20 = f32[512,1,128]{2,0,1:T(8,128)S(1)} fusion(f32[512,128]{1,0:T(8,128)S(1)} %fusion.26, s32[512]{0:T(512)S(1)} %bitcast.87, s32[512]{0:T(512)S(1)} %bitcast.75, s32[512]{0:T(512)S(1)} %bitcast.91, s32[512]{0:T(512)S(1)} %bitcast.79, s32[512]{0:T(512)S(1)} %bitcast.83, s32[512]{0:T(512)S(1)} %bitcast.71, f32[2,512,128]{2,1,0:T(8,128)S(1)} %all_gather.3), kind=kOutput, calls=%fused_computation.16 | convolution fusion | flops 407699456 | bytes 798720 | tf_op jit(solution)/shard_map/dot_general | solution.py:53
  120.4 0.4 copy.14
  120.8 17.7 %all_to_all.15 = f32[512,2,128]{2,1,0:T(2,128)S(1)} all-to-all(f32[512,2,128]{2,1,0:T(2,128)S(1)} %copy.14), channel_id=1, replica_groups=mesh['ka'=4,'rp'=8] {'rp'}, dimensions={0} | all-to-all | bytes 1048576 | tf_op jit(solution)/shard_map/all_to_all | solution.py:55
  138.6 0.3 copy.15
  138.9 1.0 copy.20
  (14 shorter events, 0.1 us)
Async XLA Ops:
  6.5 85.0 %reduce-scatter.2.cloned.1.call-start = ((), (), s32[]{:S(2)}) async-start(), calls=%async_computation.2 | async-start | bytes 1179648 | tf_op jit(solution)/shard_map/reduce_scatter | solution.py:44
  42.4 4.1 %copy-start = (bf16[128,32,1,512]{3,1,0,2:T(8,128)(2,1)S(1)}, bf16[128,32,1,512]{3,1,0,2:T(8,128)(2,1)}, u32[]{:S(2)}) copy-start(bf16[128,32,1,512]{3,1,0,2:T(8,128)(2,1)} %copy.17) | copy-start | bytes 12582916
  42.4 5.9 %copy-start.1 = (bf16[128,32,1,512]{3,1,0,2:T(8,128)(2,1)S(1)}, bf16[128,32,1,512]{3,1,0,2:T(8,128)(2,1)}, u32[]{:S(2)}) copy-start(bf16[128,32,1,512]{3,1,0,2:T(8,128)(2,1)} %copy.16) | copy-start | bytes 12582916
  50.6 5.5 %copy-start.2 = (s32[3,512]{1,0:T(4,128)S(1)}, s32[3,512]{1,0:T(4,128)}, u32[]{:S(2)}) copy-start(s32[3,512]{1,0:T(4,128)} %param.6) | copy-start | bytes 18436
  50.6 5.5 %copy-start.3 = (s32[3,512]{1,0:T(4,128)S(1)}, s32[3,512]{1,0:T(4,128)}, u32[]{:S(2)}) copy-start(s32[3,512]{1,0:T(4,128)} %param.7) | copy-start | bytes 18436
Sparse Core Ops, SparseCore 0:
  56.2 35.2 reduce-scatter.1
where the time goes:
time: 148 us; the launch traced here: 147 us
  local copies, waits for them, and re-layouts  38.3 us (26%)
  waiting for transfers between devices  35.4 us (24%)
  matrix products  30 us (20%)
  blocking collectives  28.2 us (19%)
  between operations  13.5 us (9%)
    reduce_scatter x1, waiting for transfers between devices, per_device(): reduced = lax.psum_scatter(stacked, 'rp', scatter_dimension=2, tiled=True)  35.4 us
    unnamed x12, local copies, waits for them, and re-layouts  29 us
    all_to_all x1, blocking collectives, per_device(): lax.all_to_all(combined, 'rp', split_axis=0, concat_axis=2, tiled=True)  17.7 us
    all_gather x1, blocking collectives, per_device(): fragment = lax.all_gather(reduced, 'ka', axis=1, tiled=True)  10.5 us
    slice x1, local copies, waits for them, and re-layouts, per_device(): real_in = values[:, :, 0, :]  5.88 us
    dot_general x1, matrix products, per_device(): jnp.dot(sin_part, fragment[1], precision=high, preferred_element_type=jnp...  4.77 us
    dot_general x1, matrix products, per_device(): jnp.dot(sin_part, fragment[0], precision=high, preferred_element_type=jnp...  4.55 us
    dot_general x1, matrix products, per_device(): jnp.dot(cos_part, fragment[0], precision=high, preferred_element_type=jnp...  4.52 us
  transfers between devices with their start and end apart: 1, of which 1 were waited for; matrix products, arithmetic and copies ran while one was open for 0% of the time, Pallas kernels for 0%

commit v1 on v0

--- a/solution.py
+++ b/solution.py
@@ -5,6 +5,18 @@
 from jax.sharding import PartitionSpec as P
 
 NKG = 16
+
+
+def in_blocks(shard, dim, length):
+    lengths = shard.shape
+    parts = shard.reshape(*lengths[:dim], length, lengths[dim] // length, *lengths[dim + 1 :])
+    return jnp.moveaxis(parts, dim, 0)
+
+
+def joined_along(blocks, dim):
+    shape = list(blocks.shape[1:])
+    shape[dim] *= blocks.shape[0]
+    return jnp.moveaxis(blocks, 0, dim).reshape(shape)
 
 
 def phases(left, right):
@@ -52,7 +64,14 @@
         sin_part, fragment[0], precision=high, preferred_element_type=jnp.float32
     ) + jnp.dot(cos_part, fragment[1], precision=high, preferred_element_type=jnp.float32)
     combined = jnp.stack([real_add, imag_add], axis=1)
-    moved = lax.all_to_all(combined, "rp", split_axis=0, concat_axis=2, tiled=True)
+    size, index = (lax.axis_size("rp"), lax.axis_index("rp"))
+    pieces = in_blocks(combined, 0, size)
+    outs = [pieces[index]]
+    for step in range(1, size):
+        sent = pieces[index ^ step]
+        outs.append(lax.ppermute(sent, "rp", [(i, i ^ step) for i in range(size)]))
+    pieces = jnp.stack(outs)[index ^ jnp.arange(size)]
+    moved = joined_along(pieces, 2)
     return moved.reshape(moved.shape[0], 2 * waves * entries)
 
 

time: 148 us -> 143 us (0.966)
  blocking collectives: 28.2 us -> 10.2 us
  waiting for transfers between devices: 35.4 us -> 43 us
  starting transfers between devices: 0.01 us -> 5.92 us
    all_to_all x1 -> x0, blocking collectives: 17.7 us -> none  [per_device(): lax.all_to_all(combined, 'rp', split_axis=0, concat_axis=2, tiled=True)]
    ppermute x0 -> x7, waiting for transfers between devices: none -> 7.34 us  [per_device(): outs.append(lax.ppermute(sent, 'rp', [(i, i ^ step) for i in range(size)]))]
    ppermute x0 -> x7, starting transfers between devices: none -> 5.92 us  [per_device(): outs.append(lax.ppermute(sent, 'rp', [(i, i ^ step) for i in range(size)]))]
    unnamed x12 -> x18, local copies, waits for them, and re-layouts: 29 us -> 29 us
  transfers between devices with their start and end apart: 1 -> 8, of which waited for: 1 -> 6; matrix products, arithmetic and copies ran while one was open for 0% -> 0% of each run, Pallas kernels for 0% -> 0%
where the time goes in v1:
time: 143 us; the launch traced here: 142 us
  waiting for transfers between devices  43 us (30%)
  local copies, waits for them, and re-layouts  38.5 us (27%)
  matrix products  30 us (21%)
  between operations  13.6 us (10%)
  blocking collectives  10.2 us (7%)
  starting transfers between devices  5.92 us (4%)
    reduce_scatter x1, waiting for transfers between devices, per_device(): reduced = lax.psum_scatter(stacked, 'rp', scatter_dimension=2, tiled=True)  35.7 us
    unnamed x18, local copies, waits for them, and re-layouts  29 us
    all_gather x1, blocking collectives, per_device(): fragment = lax.all_gather(reduced, 'ka', axis=1, tiled=True)  10.2 us
    ppermute x7, waiting for transfers between devices, per_device(): outs.append(lax.ppermute(sent, 'rp', [(i, i ^ step) for i in range(size)]))  7.34 us
    ppermute x7, starting transfers between devices, per_device(): outs.append(lax.ppermute(sent, 'rp', [(i, i ^ step) for i in range(size)]))  5.92 us
    slice x1, local copies, waits for them, and re-layouts, per_device(): real_in = values[:, :, 0, :]  5.88 us
    dot_general x1, matrix products, per_device(): jnp.dot(cos_part, fragment[1], precision=high, preferred_element_type=jnp...  4.74 us
    dot_general x1, matrix products, per_device(): jnp.dot(sin_part, fragment[1], precision=high, preferred_element_type=jnp...  4.56 us
  transfers between devices with their start and end apart: 8, of which 6 were waited for; matrix products, arithmetic and copies ran while one was open for 0% of the time, Pallas kernels for 0%

profile of v1, /device:TPU:0, one launch (start us, length us, event | category | flops | bytes accessed | tf_op | source)
XLA Modules:
  0.0 142.5 jit_solution(16367512560348488426)
XLA Ops:
  6.5 0.8 slice_bitcast_fusion.8
  7.3 1.0 slice_reduce_fusion.2
  8.3 12.1 %copy.7 = bf16[128,32,1024]{0,2,1:T(8,128)(2,1)} copy(bf16[128,32,1024]{2,1,0:T(8,128)(2,1)} %param.5) | data formatting | bytes 16777216 | tf_op args[0]
  20.4 5.9 %fusion.67 = (bf16[128,32,1,512]{0,3,2,1:T(8,128)(2,1)}, bf16[128,32,1,512]{0,3,2,1:T(8,128)(2,1)}) fusion(bf16[128,32,2,512]{0,3,2,1:T(8,128)(2,1)} %bitcast.91), kind=kLoop, calls=%fused_computation.104 | loop fusion | bytes 16777216 | tf_op jit(solution)/shard_map/slice | solution.py:44
  26.3 7.9 %copy.12 = bf16[128,32,1,512]{3,1,0,2:T(8,128)(2,1)} copy(bf16[128,32,1,512]{0,3,2,1:T(8,128)(2,1)} %get-tuple-element.11) | data formatting | bytes 8388608
  34.4 8.0 %copy.11 = bf16[128,32,1,512]{3,1,0,2:T(8,128)(2,1)} copy(bf16[128,32,1,512]{0,3,2,1:T(8,128)(2,1)} %get-tuple-element.10) | data formatting | bytes 8388608
  42.4 4.1 %fusion.2 = f32[2,128,512]{2,0,1:T(2,128)S(1)} fusion(bf16[128,32,1,512]{3,1,0,2:T(8,128)(2,1)} %copy.12, f32[2,32]{1,0:T(2,128)S(1)} %get-tuple-element.8), kind=kOutput, calls=%fused_computation.3 | convolution fusion | flops 50331648 | bytes 4718848 | tf_op jit(solution)/shard_map/qr,erm->eqm/dot_general | solution.py:46
  46.5 1.8 %fusion = f32[2,128,512]{2,0,1:T(2,128)S(1)} fusion(bf16[128,32,1,512]{3,1,0,2:T(8,128)(2,1)S(1)} %copy-done, f32[2,32]{1,0:T(2,128)S(1)} %cos.7), kind=kOutput, calls=%fused_computation.1 | convolution fusion | flops 50331648 | bytes 4718848 | tf_op jit(solution)/shard_map/qr,erm->eqm/dot_general | solution.py:49
  48.3 1.8 %fusion.11 = f32[128,2,512]{2,1,0:T(2,128)S(1)} fusion(f32[2,128,512]{2,0,1:T(2,128)S(1)} %fusion.2, bf16[128,32,1,512]{3,1,0,2:T(8,128)(2,1)S(1)} %copy-done.1, f32[2,32]{1,0:T(2,128)S(1)} %cos.7), kind=kOutput, calls=%fused_computation.13 | convolution fusion | flops 50462720 | bytes 5243136 | tf_op jit(solution)/shard_map/qr,erm->eqm/dot_general | solution.py:46
  50.5 3.9 %fusion.17 = f32[128,2,512]{2,1,0:T(2,128)S(1)} fusion(f32[2,128,512]{2,0,1:T(2,128)S(1)} %fusion, bf16[128,32,1,512]{3,1,0,2:T(8,128)(2,1)} %copy.11, f32[2,32]{1,0:T(2,128)S(1)} %get-tuple-element.8), kind=kOutput, calls=%fused_computation.15 | convolution fusion | flops 50462720 | bytes 5243136 | tf_op jit(solution)/shard_map/qr,erm->eqm/dot_general | solution.py:49
  54.9 1.0 pad_maximum_fusion
  56.1 35.7 %reduce-scatter.2.cloned.1.call-done = f32[2,128,128]{2,1,0:T(8,128)} async-done(((f32[2,128,1024]{2,1,0:T(8,128)}), f32[2,128,128]{2,1,0:T(8,128)}) %reduce-scatter.2.cloned.1.call-update) | async-done | bytes 131088 | tf_op jit(solution)/shard_map/reduce_scatter | solution.py:56
  91.8 10.2 %all_gather.3 = f32[2,512,128]{2,1,0:T(8,128)S(1)} all-gather(f32[2,128,128]{2,1,0:T(8,128)} %reduce-scatter.2.cloned.1.call-done), channel_id=1, replica_groups=mesh['ka'=4,'rp'=8] {'ka'}, dimensions={1}, use_global_device_ids=true | all-gather | bytes 655360 | tf_op jit(solution)/shard_map/all_gather | solution.py:57
  102.0 4.6 %fusion.24 = f32[512,128]{1,0:T(8,128)S(1)} fusion(s32[512]{0:T(512)S(1)} %bitcast.114, s32[512]{0:T(512)S(1)} %bitcast.102, s32[512]{0:T(512)S(1)} %bitcast.118, s32[512]{0:T(512)S(1)} %bitcast.106, s32[512]{0:T(512)S(1)} %bitcast.110, s32[512]{0:T(512)S(1)} %bitcast.98, f32[2,512,128]{2,1,0:T(8,128)S(1)} %all_gather.3), kind=kOutput, calls=%fused_computation.42 | convolution fusion | flops 407633920 | bytes 536576 | tf_op jit(solution)/shard_map/dot_general | solution.py:63
  106.5 4.5 %fusion.23 = f32[512,128]{1,0:T(8,128)S(1)} fusion(s32[512]{0:T(512)S(1)} %bitcast.115, s32[512]{0:T(512)S(1)} %bitcast.103, s32[512]{0:T(512)S(1)} %bitcast.119, s32[512]{0:T(512)S(1)} %bitcast.107, s32[512]{0:T(512)S(1)} %bitcast.111, s32[512]{0:T(512)S(1)} %bitcast.99, f32[2,512,128]{2,1,0:T(8,128)S(1)} %all_gather.3), kind=kOutput, calls=%fused_computation.41 | convolution fusion | flops 407633920 | bytes 536576 | tf_op jit(solution)/shard_map/dot_general | solution.py:60
  111.0 4.7 %convolution_add_fusion = f32[512,128]{1,0:T(8,128)S(1)} fusion(f32[512,128]{1,0:T(8,128)S(1)} %fusion.24, s32[512]{0:T(512)S(1)} %bitcast.116, s32[512]{0:T(512)S(1)} %bitcast.104, s32[512]{0:T(512)S(1)} %bitcast.120, s32[512]{0:T(512)S(1)} %bitcast.108, s32[512]{0:T(512)S(1)} %bitcast.112, s32[512]{0:T(512)S(1)} %bitcast.100, ...), kind=kOutput, calls=%fused_computation.32 | convolution fusion | flops 407699456 | bytes 798720 | tf_op jit(solution)/shard_map/dot_general | solution.py:65
  115.8 4.6 %convolution_subtract_fusion = f32[512,128]{1,0:T(8,128)S(1)} fusion(f32[512,128]{1,0:T(8,128)S(1)} %fusion.23, s32[512]{0:T(512)S(1)} %bitcast.117, s32[512]{0:T(512)S(1)} %bitcast.105, s32[512]{0:T(512)S(1)} %bitcast.121, s32[512]{0:T(512)S(1)} %bitcast.109, s32[512]{0:T(512)S(1)} %bitcast.113, s32[512]{0:T(512)S(1)} %bitcast.101, ...), kind=kOutput, calls=%fused_computation.33 | convolution fusion | flops 407699456 | bytes 798720 | tf_op jit(solution)/shard_map/dot_general | solution.py:62
  120.6 1.5 %collective-permute-start.1 = (f32[64,2,128]{2,0,1:T(8,128)S(1)}, f32[64,2,128]{2,0,1:T(8,128)S(1)}, u32[]{:S(2)}, u32[]{:S(2)}) collective-permute-start(f32[64,2,128]{2,0,1:T(8,128)S(1)} %get-tuple-element.15), channel_id=1, source_target_pairs={{0,2},{1,3},{2,0},{3,1},{4,6},{5,7},{6,4},{7,5},{8,10},{9,11},{10,... | collective-permute-start | bytes 196616 | tf_op jit(solution)/shard_map/ppermute | solution.py:72
  122.5 2.5 %collective-permute-start.3 = (f32[64,2,128]{2,0,1:T(8,128)S(1)}, f32[64,2,128]{2,0,1:T(8,128)S(1)}, u32[]{:S(2)}, u32[]{:S(2)}) collective-permute-start(f32[64,2,128]{2,0,1:T(8,128)S(1)} %get-tuple-element.17), channel_id=1, source_target_pairs={{0,4},{1,5},{2,6},{3,7},{4,0},{5,1},{6,2},{7,3},{8,12},{9,13},{10,... | collective-permute-start | bytes 196616 | tf_op jit(solution)/shard_map/ppermute | solution.py:72
  125.0 0.9 collective-permute-start.5
  125.8 2.3 %collective-permute-done.1 = f32[64,2,128]{2,0,1:T(8,128)S(1)} collective-permute-done((f32[64,2,128]{2,0,1:T(8,128)S(1)}, f32[64,2,128]{2,0,1:T(8,128)S(1)}, u32[]{:S(2)}, u32[]{:S(2)}) %collective-permute-start.1) | collective-permute-done | bytes 65568 | tf_op jit(solution)/shard_map/ppermute | solution.py:72
  129.1 2.2 %collective-permute-done.5 = f32[64,2,128]{2,0,1:T(8,128)S(1)} collective-permute-done((f32[64,2,128]{2,0,1:T(8,128)S(1)}, f32[64,2,128]{2,0,1:T(8,128)S(1)}, u32[]{:S(2)}, u32[]{:S(2)}) %collective-permute-start.5) | collective-permute-done | bytes 65568 | tf_op jit(solution)/shard_map/ppermute | solution.py:72
  131.3 2.5 %collective-permute-done.6 = f32[64,2,128]{2,0,1:T(8,128)S(1)} collective-permute-done((f32[64,2,128]{2,0,1:T(8,128)S(1)}, f32[64,2,128]{2,0,1:T(8,128)S(1)}, u32[]{:S(2)}, u32[]{:S(2)}) %collective-permute-start.6) | collective-permute-done | bytes 65568 | tf_op jit(solution)/shard_map/ppermute | solution.py:72
  134.7 1.0 copy.15
  (37 shorter events, 3.5 us)
Async XLA Ops:
  6.5 85.3 %reduce-scatter.2.cloned.1.call-start = ((), (), s32[]{:S(2)}) async-start(), calls=%async_computation.1 | async-start | bytes 1179648 | tf_op jit(solution)/shard_map/reduce_scatter | solution.py:56
  42.4 4.1 %copy-start = (bf16[128,32,1,512]{3,1,0,2:T(8,128)(2,1)S(1)}, bf16[128,32,1,512]{3,1,0,2:T(8,128)(2,1)}, u32[]{:S(2)}) copy-start(bf16[128,32,1,512]{3,1,0,2:T(8,128)(2,1)} %copy.12) | copy-start | bytes 12582916
  42.4 5.9 %copy-start.1 = (bf16[128,32,1,512]{3,1,0,2:T(8,128)(2,1)S(1)}, bf16[128,32,1,512]{3,1,0,2:T(8,128)(2,1)}, u32[]{:S(2)}) copy-start(bf16[128,32,1,512]{3,1,0,2:T(8,128)(2,1)} %copy.11) | copy-start | bytes 12582916
  50.5 5.6 %copy-start.2 = (s32[3,512]{1,0:T(4,128)S(1)}, s32[3,512]{1,0:T(4,128)}, u32[]{:S(2)}) copy-start(s32[3,512]{1,0:T(4,128)} %param.6) | copy-start | bytes 18436
  50.5 5.6 %copy-start.3 = (s32[3,512]{1,0:T(4,128)S(1)}, s32[3,512]{1,0:T(4,128)}, u32[]{:S(2)}) copy-start(s32[3,512]{1,0:T(4,128)} %param.7) | copy-start | bytes 18436
  120.4 4.6 %collective-permute-start = (f32[64,2,128]{2,0,1:T(8,128)S(1)}, f32[64,2,128]{2,0,1:T(8,128)S(1)}, u32[]{:S(2)}, u32[]{:S(2)}) collective-permute-start(f32[64,2,128]{2,0,1:T(8,128)S(1)} %get-tuple-element.14), channel_id=1, source_target_pairs={{0,1},{1,0},{2,3},{3,2},{4,5},{5,4},{6,7},{7,6},{8,9},{9,8},{10,11... | collective-permute-start | bytes 196616 | tf_op jit(solution)/shard_map/ppermute | solution.py:72
  120.5 8.6 %collective-permute-start.4 = (f32[64,2,128]{2,0,1:T(8,128)S(1)}, f32[64,2,128]{2,0,1:T(8,128)S(1)}, u32[]{:S(2)}, u32[]{:S(2)}) collective-permute-start(f32[64,2,128]{2,0,1:T(8,128)S(1)} %get-tuple-element.19), channel_id=1, source_target_pairs={{0,5},{1,4},{2,7},{3,6},{4,1},{5,0},{6,3},{7,2},{8,13},{9,12},{10,... | collective-permute-start | bytes 196616 | tf_op jit(solution)/shard_map/ppermute | solution.py:72
  120.6 7.6 %collective-permute-start.1 = (f32[64,2,128]{2,0,1:T(8,128)S(1)}, f32[64,2,128]{2,0,1:T(8,128)S(1)}, u32[]{:S(2)}, u32[]{:S(2)}) collective-permute-start(f32[64,2,128]{2,0,1:T(8,128)S(1)} %get-tuple-element.15), channel_id=1, source_target_pairs={{0,2},{1,3},{2,0},{3,1},{4,6},{5,7},{6,4},{7,5},{8,10},{9,11},{10,... | collective-permute-start | bytes 196616 | tf_op jit(solution)/shard_map/ppermute | solution.py:72
  122.1 6.6 %collective-permute-start.2 = (f32[64,2,128]{2,0,1:T(8,128)S(1)}, f32[64,2,128]{2,0,1:T(8,128)S(1)}, u32[]{:S(2)}, u32[]{:S(2)}) collective-permute-start(f32[64,2,128]{2,0,1:T(8,128)S(1)} %get-tuple-element.16), channel_id=1, source_target_pairs={{0,3},{1,2},{2,1},{3,0},{4,7},{5,6},{6,5},{7,4},{8,11},{9,10},{10,... | collective-permute-start | bytes 196616 | tf_op jit(solution)/shard_map/ppermute | solution.py:72
  122.5 6.6 %collective-permute-start.3 = (f32[64,2,128]{2,0,1:T(8,128)S(1)}, f32[64,2,128]{2,0,1:T(8,128)S(1)}, u32[]{:S(2)}, u32[]{:S(2)}) collective-permute-start(f32[64,2,128]{2,0,1:T(8,128)S(1)} %get-tuple-element.17), channel_id=1, source_target_pairs={{0,4},{1,5},{2,6},{3,7},{4,0},{5,1},{6,2},{7,3},{8,12},{9,13},{10,... | collective-permute-start | bytes 196616 | tf_op jit(solution)/shard_map/ppermute | solution.py:72
  125.0 6.3 %collective-permute-start.5 = (f32[64,2,128]{2,0,1:T(8,128)S(1)}, f32[64,2,128]{2,0,1:T(8,128)S(1)}, u32[]{:S(2)}, u32[]{:S(2)}) collective-permute-start(f32[64,2,128]{2,0,1:T(8,128)S(1)} %get-tuple-element.18), channel_id=1, source_target_pairs={{0,6},{1,7},{2,4},{3,5},{4,2},{5,3},{6,0},{7,1},{8,14},{9,15},{10,... | collective-permute-start | bytes 196616 | tf_op jit(solution)/shard_map/ppermute | solution.py:72
  128.2 5.6 %collective-permute-start.6 = (f32[64,2,128]{2,0,1:T(8,128)S(1)}, f32[64,2,128]{2,0,1:T(8,128)S(1)}, u32[]{:S(2)}, u32[]{:S(2)}) collective-permute-start(f32[64,2,128]{2,0,1:T(8,128)S(1)} %get-tuple-element.12), channel_id=1, source_target_pairs={{0,7},{1,6},{2,5},{3,4},{4,3},{5,2},{6,1},{7,0},{8,15},{9,14},{10,... | collective-permute-start | bytes 196616 | tf_op jit(solution)/shard_map/ppermute | solution.py:72
Sparse Core Ops, SparseCore 0:
  56.1 35.6 reduce-scatter.1
